TPU v7x, 256 devices: a whole 4x4x8 slice. The times are simulated.
256 devices in a mesh: layer: 2 (over z_lo), row: 8 (over y, core), col: 16 (over z_hi, x).
Axes of the slice: x: 4, y: 4, z: 8 (z_hi: 4, z_lo: 2; z = z_hi * 2 + z_lo), core: 2. Of those that a mesh axis runs over, the one named last changes fastest.
Arguments:
- matrix: float32 [16384, 16384], P('row', 'col'), may hold values from -1.5 to 1.5, as said below
Outputs:
- square_panel: float32 [16384, 512], P('row', 'layer')
- new_panel: float32 [16384, 512], P('row', 'layer')
Inputs may be any that keep to these rules, and one draw needn't show every extreme that they name: `matrix`: entries off the diagonal are of order 0.5 / sqrt(16384); the diagonal's magnitudes lie between 0.6 and 1 with either sign.
All inputs are finite; a program needn't handle non-finite values.
Results may differ from a plain program's by a relative error of at most 0.000076.
Values sent between devices are 32-bit elements; how exact they have to be, the bound alone decides.
A program may use at most 128 MiB of HBM per device.

v0:
```python
import jax
import jax.numpy as jnp
from jax import lax
from jax.sharding import PartitionSpec as P

PW = 512


def from_root(shard, axis, root):
    mine = lax.axis_index(axis) == root
    return lax.psum(jnp.where(mine, shard, jnp.zeros_like(shard)), axis)


def matmul_high(left_side, right_side):
    return jnp.dot(
        left_side, right_side, precision=lax.Precision.HIGHEST, preferred_element_type=jnp.float32
    )


def body(matrix):
    block_cols = matrix.shape[1]
    layers = lax.axis_size("layer")
    col_ratio = lax.axis_size("col") // lax.axis_size("row")
    col_index = lax.axis_index("col")
    layer_index = lax.axis_index("layer")
    half_width = PW // layers
    root_row = col_index // col_ratio
    offset = col_index % col_ratio * block_cols
    panel_full = from_root(matrix[:, :PW], "col", 0)
    own_cols = lax.dynamic_slice_in_dim(panel_full, layer_index * half_width, half_width, 1)
    depth_rows = block_cols // layers
    first_row = offset + layer_index * depth_rows
    panel_slab = from_root(
        lax.dynamic_slice_in_dim(panel_full, first_row, depth_rows, 0), "row", root_row
    )
    local_cols = lax.dynamic_slice_in_dim(matrix, layer_index * depth_rows, depth_rows, 1)
    square_full = lax.psum(matmul_high(local_cols, panel_slab), ("layer", "col"))
    square_slab = from_root(
        lax.dynamic_slice_in_dim(square_full, first_row, depth_rows, 0), "row", root_row
    )
    update = lax.psum_scatter(
        matmul_high(local_cols, square_slab), "layer", scatter_dimension=1, tiled=True
    )
    update = lax.psum(update, "col")
    square = lax.dynamic_slice_in_dim(square_full, layer_index * half_width, half_width, 1)
    new_panel = (3.0 * own_cols - update) * 0.5
    return (square, new_panel)


def solution(mesh):
    placed = (P("row", "col"),)
    return jax.shard_map(
        body,
        mesh=mesh,
        in_specs=placed,
        out_specs=(P("row", "layer"), P("row", "layer")),
        check_vma=False,
    )
```

profile of v0, /device:TPU:16, one launch (start us, length us, event | category | flops | bytes accessed | tf_op | source)
XLA Modules:
  0.0 809.4 jit_solution(460881230599396828)
XLA Ops:
  7.2 0.0 all-reduce.6.cloned.1.call-start
  7.2 4.6 slice_select_fusion
  11.9 0.0 all-reduce.6.cloned.1.call-update
  11.9 0.0 all-reduce.8.cloned.1.call-start
  12.0 224.7 %all-reduce.6.cloned.1.call-done = f32[2048,512]{1,0:T(8,128)} async-done(((f32[2048,512]{1,0:T(8,128)}), f32[2048,512]{1,0:T(8,128)}) %all-reduce.6.cloned.1.call-update) | async-done | bytes 4194320 | tf_op jit(solution)/shard_map/psum | solution.py:11
  236.6 2.3 dynamic-slice_select_fusion.1
  238.9 0.0 all-reduce.8.cloned.1.call-update
  239.0 0.0 all-reduce.10.cloned.1.call-start
  239.0 61.4 %all-reduce.8.cloned.1.call-done = f32[512,512]{1,0:T(8,128)} async-done(((f32[512,512]{1,0:T(8,128)}), f32[512,512]{1,0:T(8,128)}) %all-reduce.8.cloned.1.call-update) | async-done | bytes 1048592 | tf_op jit(solution)/shard_map/psum | solution.py:11
  300.4 10.1 %fusion.2 = f32[2048,512]{1,0:T(8,128)} fusion(f32[512,512]{1,0:T(8,128)} %all-reduce.8.cloned.1.call-done, f32[2048,1024]{1,0:T(8,128)} %param.1, s32[]{:T(128)S(6)} %select_n.42), kind=kOutput, calls=%fused_computation.3 | convolution fusion | flops 6442450944 | bytes 9437188 | tf_op jit(solution)/shard_map/dot_general | solution.py:15
  310.5 0.0 all-reduce.10.cloned.1.call-update
  310.5 0.0 all-reduce.12.cloned.1.call-start
  310.6 167.7 %all-reduce.10.cloned.1.call-done = f32[2048,512]{1,0:T(8,128)} async-done(((f32[2048,512]{1,0:T(8,128)}), f32[2048,512]{1,0:T(8,128)}) %all-reduce.10.cloned.1.call-update) | async-done | bytes 4194320 | tf_op jit(solution)/shard_map/psum | solution.py:37
  478.2 2.3 dynamic-slice_select_fusion
  480.5 0.0 all-reduce.12.cloned.1.call-update
  480.6 0.0 reduce-scatter.2.cloned.1.call-start
  480.6 61.5 %all-reduce.12.cloned.1.call-done = f32[512,512]{1,0:T(8,128)} async-done(((f32[512,512]{1,0:T(8,128)}), f32[512,512]{1,0:T(8,128)}) %all-reduce.12.cloned.1.call-update) | async-done | bytes 1048592 | tf_op jit(solution)/shard_map/psum | solution.py:11
  542.1 10.1 %fusion = f32[2048,512]{1,0:T(8,128)} fusion(f32[512,512]{1,0:T(8,128)} %all-reduce.12.cloned.1.call-done, f32[2048,1024]{1,0:T(8,128)} %param.1, s32[]{:T(128)S(6)} %select_n.42), kind=kOutput, calls=%fused_computation.1 | convolution fusion | flops 6442450944 | bytes 9437188 | tf_op jit(solution)/shard_map/dot_general | solution.py:15
  552.2 0.0 reduce-scatter.2.cloned.1.call-update
  552.2 0.0 all-reduce.14.cloned.1.call-start
  552.2 62.9 %reduce-scatter.2.cloned.1.call-done = f32[2048,256]{1,0:T(8,128)} async-done(((f32[2048,512]{1,0:T(8,128)}), f32[2048,256]{1,0:T(8,128)}) %reduce-scatter.2.cloned.1.call-update) | async-done | bytes 2097168 | tf_op jit(solution)/shard_map/reduce_scatter | solution.py:41
  615.2 0.0 all-reduce.14.cloned.1.call-update
  615.2 3.0 constant_dynamic-slice_fusion
  618.3 180.5 %all-reduce.14.cloned.1.call-done = f32[2048,256]{1,0:T(8,128)} async-done(((f32[2048,256]{1,0:T(8,128)}), f32[2048,256]{1,0:T(8,128)}) %all-reduce.14.cloned.1.call-update) | async-done | bytes 2097168 | tf_op jit(solution)/shard_map/psum | solution.py:44
  798.7 3.8 subtract_multiply_fusion
Async XLA Ops:
  7.2 229.5 %all-reduce.6.cloned.1.call-start = ((), (), s32[]{:S(2)}) async-start(), calls=%async_computation.1 | async-start | bytes 8388608 | tf_op jit(solution)/shard_map/psum | solution.py:11
  11.9 288.5 %all-reduce.8.cloned.1.call-start = ((), (), s32[]{:S(2)}) async-start(), calls=%async_computation.2 | async-start | bytes 2097152 | tf_op jit(solution)/shard_map/psum | solution.py:11
  239.0 239.3 %all-reduce.10.cloned.1.call-start = ((), (), s32[]{:S(2)}) async-start(), calls=%async_computation.3 | async-start | bytes 8388608 | tf_op jit(solution)/shard_map/psum | solution.py:37
  310.5 231.6 %all-reduce.12.cloned.1.call-start = ((), (), s32[]{:S(2)}) async-start(), calls=%async_computation.4 | async-start | bytes 2097152 | tf_op jit(solution)/shard_map/psum | solution.py:11
  480.6 134.6 %reduce-scatter.2.cloned.1.call-start = ((), (), s32[]{:S(2)}) async-start(), calls=%async_computation.5 | async-start | bytes 6291456 | tf_op jit(solution)/shard_map/reduce_scatter | solution.py:41
  552.2 246.5 %all-reduce.14.cloned.1.call-start = ((), (), s32[]{:S(2)}) async-start(), calls=%async_computation.6 | async-start | bytes 4194304 | tf_op jit(solution)/shard_map/psum | solution.py:44
Sparse Core Ops, SparseCore 0:
  12.0 224.5 all-reduce.5
  239.6 60.7 all-reduce.7
  310.6 167.5 all-reduce.9
  481.0 61.0 all-reduce.11
  552.3 62.8 reduce-scatter.1
  617.7 180.9 all-reduce.13
where the time goes:
time: 810 us; the launch traced here: 809 us
  waiting for transfers between devices  759 us (94%)
  matrix products  20.1 us (2%)
  between operations  14.2 us (2%)
  other arithmetic  13 us (2%)
    psum x3, waiting for transfers between devices, from_root(): return lax.psum(jnp.where(mine, shard, jnp.zeros_like(shard)), axis)  348 us
    psum x1, waiting for transfers between devices, body(): update = lax.psum(update, 'col')  180 us
    psum x1, waiting for transfers between devices, body(): lax.psum(matmul_high(local_cols, panel_slab), ('layer', 'col'))  168 us
    reduce_scatter x1, waiting for transfers between devices, body(): lax.psum_scatter(matmul_high(local_cols, square_slab), 'layer', scatter_d...  62.9 us
    dot_general x2, matrix products, matmul_high(): jnp.dot(left_side, right_side, precision=lax.Precision.HIGHEST, preferred...  20.1 us
  transfers between devices with their start and end apart: 6, of which 6 were waited for; matrix products, arithmetic and copies ran while one was open for 0% of the time, Pallas kernels for 0%

commit v1 on v0

--- a/solution.py
+++ b/solution.py
@@ -34,7 +34,7 @@
         lax.dynamic_slice_in_dim(panel_full, first_row, depth_rows, 0), "row", root_row
     )
     local_cols = lax.dynamic_slice_in_dim(matrix, layer_index * depth_rows, depth_rows, 1)
-    square_full = lax.psum(matmul_high(local_cols, panel_slab), ("layer", "col"))
+    square_full = lax.psum(lax.psum(matmul_high(local_cols, panel_slab), "layer"), "col")
     square_slab = from_root(
         lax.dynamic_slice_in_dim(square_full, first_row, depth_rows, 0), "row", root_row
     )

time: 810 us -> 990 us (1.22)
  waiting for transfers between devices: 759 us -> 938 us
    psum x1 -> x2, waiting for transfers between devices: 168 us -> 348 us  [the longest x1 225 us: body(): lax.psum(lax.psum(matmul_high(local_cols, panel_slab), 'layer'), 'col')]
  transfers between devices with their start and end apart: 6 -> 7, of which waited for: 6 -> 7; matrix products, arithmetic and copies ran while one was open for 0% -> 0% of each run, Pallas kernels for 0% -> 0%
where the time goes in v1:
time: 990 us; the launch traced here: 989 us
  waiting for transfers between devices  938 us (95%)
  matrix products  20.2 us (2%)
  between operations  14.2 us (1%)
  other arithmetic  13 us (1%)
    psum x3, waiting for transfers between devices, from_root(): return lax.psum(jnp.where(mine, shard, jnp.zeros_like(shard)), axis)  347 us
    psum x1, waiting for transfers between devices, body(): lax.psum(lax.psum(matmul_high(local_cols, panel_slab), 'layer'), 'col')  225 us
    psum x1, waiting for transfers between devices, body(): update = lax.psum(update, 'col')  180 us
    psum x1, waiting for transfers between devices, body(): lax.psum(matmul_high(local_cols, panel_slab), 'layer')  123 us
    reduce_scatter x1, waiting for transfers between devices, body(): lax.psum_scatter(matmul_high(local_cols, square_slab), 'layer', scatter_d...  62.9 us
    dot_general x2, matrix products, matmul_high(): jnp.dot(left_side, right_side, precision=lax.Precision.HIGHEST, preferred...  20.2 us
  transfers between devices with their start and end apart: 7, of which 7 were waited for; matrix products, arithmetic and copies ran while one was open for 0% of the time, Pallas kernels for 0%

profile of v1, /device:TPU:16, one launch (start us, length us, event | category | flops | bytes accessed | tf_op | source)
XLA Modules:
  0.0 989.0 jit_solution(5295545514116654973)
XLA Ops:
  7.2 0.0 all-reduce.7.cloned.1.call-start
  7.2 4.6 slice_select_fusion
  11.9 0.0 all-reduce.7.cloned.1.call-update
  11.9 0.0 all-reduce.9.cloned.1.call-start
  12.0 224.7 %all-reduce.7.cloned.1.call-done = f32[2048,512]{1,0:T(8,128)} async-done(((f32[2048,512]{1,0:T(8,128)}), f32[2048,512]{1,0:T(8,128)}) %all-reduce.7.cloned.1.call-update) | async-done | bytes 4194320 | tf_op jit(solution)/shard_map/psum | solution.py:11
  236.6 2.3 dynamic-slice_select_fusion.1
  238.9 0.0 all-reduce.9.cloned.1.call-update
  239.0 0.0 all-reduce.11.cloned.1.call-start
  239.0 61.4 %all-reduce.9.cloned.1.call-done = f32[512,512]{1,0:T(8,128)} async-done(((f32[512,512]{1,0:T(8,128)}), f32[512,512]{1,0:T(8,128)}) %all-reduce.9.cloned.1.call-update) | async-done | bytes 1048592 | tf_op jit(solution)/shard_map/psum | solution.py:11
  300.4 10.1 %fusion.2 = f32[2048,512]{1,0:T(8,128)} fusion(f32[512,512]{1,0:T(8,128)} %all-reduce.9.cloned.1.call-done, f32[2048,1024]{1,0:T(8,128)} %param.1, s32[]{:T(128)S(6)} %select_n.42), kind=kOutput, calls=%fused_computation.3 | convolution fusion | flops 6442450944 | bytes 9437188 | tf_op jit(solution)/shard_map/dot_general | solution.py:15
  310.5 0.0 all-reduce.11.cloned.1.call-update
  310.5 0.0 all-reduce.13.cloned.1.call-start
  310.6 122.6 %all-reduce.11.cloned.1.call-done = f32[2048,512]{1,0:T(8,128)} async-done(((f32[2048,512]{1,0:T(8,128)}), f32[2048,512]{1,0:T(8,128)}) %all-reduce.11.cloned.1.call-update) | async-done | bytes 4194320 | tf_op jit(solution)/shard_map/psum | solution.py:37
  433.2 0.0 all-reduce.13.cloned.1.call-update
  433.2 0.0 all-reduce.15.cloned.1.call-start
  433.3 225.3 %all-reduce.13.cloned.1.call-done = f32[2048,512]{1,0:T(8,128)} async-done(((f32[2048,512]{1,0:T(8,128)}), f32[2048,512]{1,0:T(8,128)}) %all-reduce.13.cloned.1.call-update) | async-done | bytes 4194320 | tf_op jit(solution)/shard_map/psum | solution.py:37
  658.6 2.3 dynamic-slice_select_fusion
  660.8 0.0 all-reduce.15.cloned.1.call-update
  660.9 0.0 reduce-scatter.2.cloned.1.call-start
  660.9 61.3 %all-reduce.15.cloned.1.call-done = f32[512,512]{1,0:T(8,128)} async-done(((f32[512,512]{1,0:T(8,128)}), f32[512,512]{1,0:T(8,128)}) %all-reduce.15.cloned.1.call-update) | async-done | bytes 1048592 | tf_op jit(solution)/shard_map/psum | solution.py:11
  722.2 10.1 %fusion = f32[2048,512]{1,0:T(8,128)} fusion(f32[512,512]{1,0:T(8,128)} %all-reduce.15.cloned.1.call-done, f32[2048,1024]{1,0:T(8,128)} %param.1, s32[]{:T(128)S(6)} %select_n.42), kind=kOutput, calls=%fused_computation.1 | convolution fusion | flops 6442450944 | bytes 9437188 | tf_op jit(solution)/shard_map/dot_general | solution.py:15
  732.2 0.0 reduce-scatter.2.cloned.1.call-update
  732.3 0.0 all-reduce.17.cloned.1.call-start
  732.3 62.9 %reduce-scatter.2.cloned.1.call-done = f32[2048,256]{1,0:T(8,128)} async-done(((f32[2048,512]{1,0:T(8,128)}), f32[2048,256]{1,0:T(8,128)}) %reduce-scatter.2.cloned.1.call-update) | async-done | bytes 2097168 | tf_op jit(solution)/shard_map/reduce_scatter | solution.py:41
  795.3 0.0 all-reduce.17.cloned.1.call-update
  795.3 3.0 constant_dynamic-slice_fusion
  798.3 180.0 %all-reduce.17.cloned.1.call-done = f32[2048,256]{1,0:T(8,128)} async-done(((f32[2048,256]{1,0:T(8,128)}), f32[2048,256]{1,0:T(8,128)}) %all-reduce.17.cloned.1.call-update) | async-done | bytes 2097168 | tf_op jit(solution)/shard_map/psum | solution.py:44
  978.4 3.8 subtract_multiply_fusion
Async XLA Ops:
  7.2 229.5 %all-reduce.7.cloned.1.call-start = ((), (), s32[]{:S(2)}) async-start(), calls=%async_computation.1 | async-start | bytes 8388608 | tf_op jit(solution)/shard_map/psum | solution.py:11
  11.9 288.5 %all-reduce.9.cloned.1.call-start = ((), (), s32[]{:S(2)}) async-start(), calls=%async_computation.2 | async-start | bytes 2097152 | tf_op jit(solution)/shard_map/psum | solution.py:11
  239.0 194.2 %all-reduce.11.cloned.1.call-start = ((), (), s32[]{:S(2)}) async-start(), calls=%async_computation.3 | async-start | bytes 8388608 | tf_op jit(solution)/shard_map/psum | solution.py:37
  310.5 348.0 %all-reduce.13.cloned.1.call-start = ((), (), s32[]{:S(2)}) async-start(), calls=%async_computation.4 | async-start | bytes 8388608 | tf_op jit(solution)/shard_map/psum | solution.py:37
  433.2 289.0 %all-reduce.15.cloned.1.call-start = ((), (), s32[]{:S(2)}) async-start(), calls=%async_computation.5 | async-start | bytes 2097152 | tf_op jit(solution)/shard_map/psum | solution.py:11
  660.9 134.4 %reduce-scatter.2.cloned.1.call-start = ((), (), s32[]{:S(2)}) async-start(), calls=%async_computation.6 | async-start | bytes 6291456 | tf_op jit(solution)/shard_map/reduce_scatter | solution.py:41
  732.3 246.1 %all-reduce.17.cloned.1.call-start = ((), (), s32[]{:S(2)}) async-start(), calls=%async_computation.7 | async-start | bytes 4194304 | tf_op jit(solution)/shard_map/psum | solution.py:44
Sparse Core Ops, SparseCore 0:
  12.0 224.5 all-reduce.6
  239.6 60.7 all-reduce.8
  310.7 122.4 all-reduce.10
  435.7 222.7 all-reduce.12
  661.3 60.7 all-reduce.14
  732.4 62.8 reduce-scatter.1
  797.9 180.4 all-reduce.16

commit v2 on v0

--- a/solution.py
+++ b/solution.py
@@ -41,7 +41,7 @@
     update = lax.psum_scatter(
         matmul_high(local_cols, square_slab), "layer", scatter_dimension=1, tiled=True
     )
-    update = lax.psum(update, "col")
+    update = jnp.sum(lax.all_gather(update, "col"), axis=0)
     square = lax.dynamic_slice_in_dim(square_full, layer_index * half_width, half_width, 1)
     new_panel = (3.0 * own_cols - update) * 0.5
     return (square, new_panel)

time: 810 us -> 1010 us (1.25)
  waiting for transfers between devices: 759 us -> 951 us
  other arithmetic: 13 us -> 24.5 us
    all_gather x0 -> x1, waiting for transfers between devices: none -> 373 us  [body(): update = jnp.sum(lax.all_gather(update, 'col'), axis=0)]
    psum x1 -> x0, waiting for transfers between devices: 180 us -> none  [body(): update = lax.psum(update, 'col')]
    reduce_sum x0 -> x1, other arithmetic: none -> 12.1 us  [body(): update = jnp.sum(lax.all_gather(update, 'col'), axis=0)]
where the time goes in v2:
time: 1010 us
  waiting for transfers between devices  951 us (94%)
  other arithmetic  24.5 us (2%)
  matrix products  20.1 us (2%)
  between operations  14.2 us (1%)
    all_gather x1, waiting for transfers between devices, body(): update = jnp.sum(lax.all_gather(update, 'col'), axis=0)  373 us
    psum x3, waiting for transfers between devices, from_root(): return lax.psum(jnp.where(mine, shard, jnp.zeros_like(shard)), axis)  348 us
    psum x1, waiting for transfers between devices, body(): lax.psum(matmul_high(local_cols, panel_slab), ('layer', 'col'))  168 us
    reduce_scatter x1, waiting for transfers between devices, body(): lax.psum_scatter(matmul_high(local_cols, square_slab), 'layer', scatter_d...  62.9 us
  transfers between devices with their start and end apart: 6, of which 6 were waited for; matrix products, arithmetic and copies ran while one was open for 0% of the time, Pallas kernels for 0%

profile of v2, /device:TPU:16, one launch (start us, length us, event | category | flops | bytes accessed | tf_op | source)
XLA Modules:
  0.0 1013.3 jit_solution(9647460425007924038)
XLA Ops:
  7.2 0.0 all-reduce.5.cloned.1.call-start
  7.2 4.6 slice_select_fusion
  11.8 0.0 all-reduce.5.cloned.1.call-update
  11.9 0.0 all-reduce.7.cloned.1.call-start
  11.9 224.7 %all-reduce.5.cloned.1.call-done = f32[2048,512]{1,0:T(8,128)} async-done(((f32[2048,512]{1,0:T(8,128)}), f32[2048,512]{1,0:T(8,128)}) %all-reduce.5.cloned.1.call-update) | async-done | bytes 4194320 | tf_op jit(solution)/shard_map/psum | solution.py:11
  236.6 2.3 dynamic-slice_select_fusion.1
  238.9 0.0 all-reduce.7.cloned.1.call-update
  238.9 0.0 all-reduce.9.cloned.1.call-start
  239.0 61.4 %all-reduce.7.cloned.1.call-done = f32[512,512]{1,0:T(8,128)} async-done(((f32[512,512]{1,0:T(8,128)}), f32[512,512]{1,0:T(8,128)}) %all-reduce.7.cloned.1.call-update) | async-done | bytes 1048592 | tf_op jit(solution)/shard_map/psum | solution.py:11
  300.4 10.1 fusion.2
  310.4 0.0 all-reduce.9.cloned.1.call-update
  310.5 0.0 all-reduce.11.cloned.1.call-start
  310.5 167.7 %all-reduce.9.cloned.1.call-done = f32[2048,512]{1,0:T(8,128)} async-done(((f32[2048,512]{1,0:T(8,128)}), f32[2048,512]{1,0:T(8,128)}) %all-reduce.9.cloned.1.call-update) | async-done | bytes 4194320 | tf_op jit(solution)/shard_map/psum | solution.py:37
  478.2 2.3 dynamic-slice_select_fusion
  480.5 0.0 all-reduce.11.cloned.1.call-update
  480.5 0.0 reduce-scatter.2.cloned.1.call-start
  480.5 61.5 %all-reduce.11.cloned.1.call-done = f32[512,512]{1,0:T(8,128)} async-done(((f32[512,512]{1,0:T(8,128)}), f32[512,512]{1,0:T(8,128)}) %all-reduce.11.cloned.1.call-update) | async-done | bytes 1048592 | tf_op jit(solution)/shard_map/psum | solution.py:11
  542.0 10.1 fusion
  552.1 0.0 reduce-scatter.2.cloned.1.call-update
  552.1 0.0 all-gather.3.cloned.1.call-start
  552.2 62.9 %reduce-scatter.2.cloned.1.call-done = f32[2048,256]{1,0:T(8,128)} async-done(((f32[2048,512]{1,0:T(8,128)}), f32[2048,256]{1,0:T(8,128)}) %reduce-scatter.2.cloned.1.call-update) | async-done | bytes 2097168 | tf_op jit(solution)/shard_map/reduce_scatter | solution.py:41
  615.1 0.0 all-gather.3.cloned.1.call-update
  615.2 3.0 constant_dynamic-slice_fusion
  618.2 373.0 %all-gather.3.cloned.1.call-done = f32[32768,256]{1,0:T(8,128)} async-done(((f32[2048,256]{1,0:T(8,128)}), f32[32768,256]{1,0:T(8,128)}) %all-gather.3.cloned.1.call-update) | async-done | bytes 33554448 | tf_op jit(solution)/shard_map/all_gather | solution.py:44
  991.2 12.1 %reduce_sum.9 = f32[2048,256]{1,0:T(8,128)S(1)} reduce(f32[16,2048,256]{2,1,0:T(8,128)} %bitcast.3, f32[]{:T(128)} %constant.49.clone.1), dimensions={0}, to_apply=%region_5.6 | reduce | flops 7864320 | bytes 35651588 | tf_op jit(solution)/shard_map/reduce_sum | solution.py:44
  1003.3 3.2 subtract_multiply_fusion
Async XLA Ops:
  7.2 229.5 %all-reduce.5.cloned.1.call-start = ((), (), s32[]{:S(2)}) async-start(), calls=%async_computation.1 | async-start | bytes 8388608 | tf_op jit(solution)/shard_map/psum | solution.py:11
  11.9 288.5 %all-reduce.7.cloned.1.call-start = ((), (), s32[]{:S(2)}) async-start(), calls=%async_computation.2 | async-start | bytes 2097152 | tf_op jit(solution)/shard_map/psum | solution.py:11
  238.9 239.3 %all-reduce.9.cloned.1.call-start = ((), (), s32[]{:S(2)}) async-start(), calls=%async_computation.3 | async-start | bytes 8388608 | tf_op jit(solution)/shard_map/psum | solution.py:37
  310.5 231.6 %all-reduce.11.cloned.1.call-start = ((), (), s32[]{:S(2)}) async-start(), calls=%async_computation.4 | async-start | bytes 2097152 | tf_op jit(solution)/shard_map/psum | solution.py:11
  480.5 134.6 %reduce-scatter.2.cloned.1.call-start = ((), (), s32[]{:S(2)}) async-start(), calls=%async_computation.5 | async-start | bytes 6291456 | tf_op jit(solution)/shard_map/reduce_scatter | solution.py:41
  552.1 439.1 %all-gather.3.cloned.1.call-start = ((), (), s32[]{:S(2)}) async-start(), calls=%async_computation.6 | async-start | bytes 35651584 | tf_op jit(solution)/shard_map/all_gather | solution.py:44
Sparse Core Ops, SparseCore 0:
  12.0 224.5 all-reduce.4
  239.5 60.7 all-reduce.6
  310.6 167.5 all-reduce.8
  481.0 61.0 all-reduce.10
  552.3 62.8 reduce-scatter.1
  617.4 373.7 all-gather.2
